TPU v7x, 512 devices: a whole 4x4x16 slice. The times are simulated.
512 devices in a mesh: dom: 64 (over z, x_lo, core), bin: 8 (over y, x_hi).
Axes of the slice: x: 4 (x_hi: 2, x_lo: 2; x = x_hi * 2 + x_lo), y: 4, z: 16, core: 2. Of those that a mesh axis runs over, the one named last changes fastest.
Arguments:
- dust_rho: float32 [128, 65536], P('bin', 'dom'), may hold values from 0.25 to 4
- dust_vel: float32 [2, 128, 65536], P(None, 'bin', 'dom'), may hold values from -4 to 4
- gas_rho: float32 [65536], P('dom'), may hold values from 50 to 500
- gas_vel: float32 [2, 65536], P(None, 'dom'), may hold values from -4 to 4
- normals: float32 [2, 8, 65536], P(None, None, 'dom'), may hold values from -0.24 to 0.24
- inv_volume: float32 [65536], P('dom'), may hold values from 0.75 to 3
- coag_rate: float32 [65536], P('dom'), may hold values from 0.03 to 0.3
- drag_coef: float32 [128], P('bin'), as said below
- neighbours: int32 [8, 65536], P(None, 'dom'), may hold values from -1 to 1535, as said below
- send_cells: int32 [64, 4, 128], P('dom'), may hold values from -1 to 1023, as said below
- kernel: bfloat16 [128, 128], replicated, may hold values from 0.001953125 to 0.0703125, as said below
- redistrib: bfloat16 [128, 128], replicated, may hold values from -0.5 to 0.5
Outputs:
- dust_rho_out: float32 [128, 65536], P('bin', 'dom')
- dust_vel_out: float32 [2, 128, 65536], P(None, 'bin', 'dom')
- gas_vel_out: float32 [2, 65536], P(None, 'dom')
Inputs may be any that keep to these rules, and one draw needn't show every extreme that they name: Row send_cells[d, j] lists distinct cells of domain d, then -1 in the remaining slots; every row has 32 or more cells, and all rows of some domain are full. `neighbours`: an entry is -1, another local cell of the same domain, or 1024 + j * 128 + p for a ghost slot p that the sending domain fills; slot 0 of every cell is valid. `drag_coef`: Positive. `kernel`: positive and symmetric.
All inputs are finite; a program needn't handle non-finite values.
Results may differ from a plain program's by a relative error of at most 0.0048.
Values may be sent and summed in bfloat16 or wider, within the bound.
A program may use at most 64 MiB of HBM per device.

v0:
```python
import jax
import jax.numpy as jnp
from jax import lax
from jax.sharding import PartitionSpec as P

OFFSETS = (1, -1, 2, -2)


def from_behind(value, axis, steps):
    count = lax.axis_size(axis)
    pairs = [(source, (source + steps) % count) for source in range(count)]
    return lax.ppermute(value, axis, pairs)


def minmod(first, second):
    return 0.5 * (jnp.sign(first) + jnp.sign(second)) * jnp.minimum(jnp.abs(first), jnp.abs(second))


def advect(state, extended_rows, faces, face_normals, inv_vol):
    density = state[0]
    vel_x = state[1]
    vel_y = state[2]
    bin_rows = density.shape[0]
    cell_count = density.shape[1]
    face_count = faces.shape[0]
    valid_all = faces >= 0
    safe_all = jnp.maximum(faces, 0).reshape(face_count * cell_count)
    picked = jnp.take(extended_rows, safe_all, axis=0)
    picked = picked.reshape(face_count, cell_count, 3, bin_rows)
    picked = jnp.transpose(picked, (0, 2, 3, 1))
    total_mean = jnp.zeros_like(density)
    valid_count = jnp.zeros(density.shape[1:], jnp.float32)
    for face in range(face_count):
        valid = valid_all[face]
        total_mean = total_mean + jnp.where(valid, picked[face, 0], 0.0)
        valid_count = valid_count + valid.astype(jnp.float32)
    neighbour_mean = total_mean / valid_count
    flux_total = jnp.zeros_like(density)
    for face in range(face_count):
        valid = valid_all[face]
        other = picked[face, 0]
        speed = 0.5 * (
            (vel_x + picked[face, 1]) * face_normals[0, face]
            + (vel_y + picked[face, 2]) * face_normals[1, face]
        )
        limited = minmod(other - density, density - neighbour_mean)
        flux = jnp.maximum(speed, 0.0) * (density + 0.5 * limited) + jnp.minimum(speed, 0.0) * (
            other - 0.5 * limited
        )
        flux_total = flux_total + jnp.where(valid, flux, 0.0)
    return density - inv_vol * flux_total


def body(
    dust_rho,
    dust_vel,
    gas_rho,
    gas_vel,
    normals,
    inv_volume,
    coag_rate,
    drag_coef,
    neighbours,
    send_cells,
    kernel,
    redistrib,
):
    own_rows = dust_rho.shape[0]
    cell_count = dust_rho.shape[1]
    coupling = drag_coef[:, None] * gas_rho[None, :]
    share = coupling / (1.0 + coupling)
    weight = dust_rho / gas_rho[None, :] * share
    partial_sums = jnp.stack(
        [
            jnp.sum(weight, axis=0),
            jnp.sum(weight * dust_vel[0], axis=0),
            jnp.sum(weight * dust_vel[1], axis=0),
        ]
    )
    totals = lax.psum(partial_sums, "bin")
    gas_new = (gas_vel + totals[1:]) / (1.0 + totals[0])
    dust_vel_new = (dust_vel + coupling[None] * gas_new[:, None, :]) / (1.0 + coupling[None])
    state = jnp.concatenate([dust_rho[None], dust_vel_new], axis=0)
    state_rows = jnp.transpose(state.reshape(3 * own_rows, cell_count))
    blocks = [state_rows]
    for direction, offset in enumerate(OFFSETS):
        index = send_cells[0, direction]
        chosen = (
            jnp.take(state_rows, jnp.maximum(index, 0), axis=0)
            * (index >= 0).astype(jnp.float32)[:, None]
        )
        blocks.append(from_behind(chosen, "dom", offset))
    extended_rows = jnp.concatenate(blocks, axis=0)
    moved = advect(state, extended_rows, neighbours, normals, inv_volume)
    rounded = moved.astype(jnp.bfloat16)
    first_bin = lax.axis_index("bin") * own_rows
    kernel_rows = lax.dynamic_slice_in_dim(kernel, first_bin, own_rows, 0)
    columns = kernel_rows
    collide = jnp.dot(
        columns,
        lax.all_gather(rounded, "bin", axis=0, tiled=True),
        preferred_element_type=jnp.float32,
    )
    loss = (coag_rate[None, :] * rounded.astype(jnp.float32) * collide).astype(jnp.bfloat16)
    redis_rows = lax.dynamic_slice_in_dim(redistrib, first_bin, own_rows, 0)
    columns = redis_rows
    gain = jnp.dot(
        columns, lax.all_gather(loss, "bin", axis=0, tiled=True), preferred_element_type=jnp.float32
    )
    dust_rho_out = moved - loss.astype(jnp.float32) + gain
    return (dust_rho_out, dust_vel_new, gas_new)


def solution(mesh):
    placed = (
        P("bin", "dom"),
        P(None, "bin", "dom"),
        P("dom"),
        P(None, "dom"),
        P(None, None, "dom"),
        P("dom"),
        P("dom"),
        P("bin"),
        P(None, "dom"),
        P("dom", None, None),
        P(),
        P(),
    )
    return jax.shard_map(
        body,
        mesh=mesh,
        in_specs=placed,
        out_specs=(P("bin", "dom"), P(None, "bin", "dom"), P(None, "dom")),
        check_vma=False,
    )
```

profile of v0, /device:TPU:98, one launch (start us, length us, event | category | flops | bytes accessed | tf_op | source)
XLA Modules:
  0.0 177.4 jit_solution(4021776785599090148)
XLA Ops:
  0.6 0.8 compare_and_fusion
  1.5 0.8 fusion.65
  2.3 1.0 broadcast_multiply_fusion
  3.3 0.9 fusion.51
  4.2 41.3 %psum.7 = f32[3,1024]{1,0:T(4,128)S(1)} all-reduce(f32[3,1024]{1,0:T(4,128)S(1)} %pad_maximum_fusion.1), channel_id=1, replica_groups=mesh['dom'=64,'bin'=8] {'bin'}, use_global_device_ids=true, to_apply=%region_3.0 | all-reduce | flops 3072 | bytes 24576 | tf_op jit(solution)/shard_map/psum | solution.py:80
  45.5 0.7 fusion.52
  46.2 0.9 add_divide_fusion
  47.2 0.9 pad_maximum_fusion
  48.1 0.2 copy.28
  48.3 0.6 gather_fusion.1
  48.9 0.1 select_multiply_fusion.3
  49.0 1.9 %collective-permute-start = (f32[128,48]{1,0:T(8,128)S(1)}, f32[128,48]{1,0:T(8,128)S(1)}, u32[]{:S(2)}, u32[]{:S(2)}) collective-permute-start(f32[128,48]{1,0:T(8,128)S(1)} %select_multiply_fusion.3), channel_id=1, source_target_pairs={{0,8},{8,16},{16,24},{24,32},{32,40},{40,48},{48,56},{56,64},{64,7... | collective-permute-start | bytes 73736 | tf_op jit(solution)/shard_map/ppermute | solution.py:12
  51.0 0.6 gather_fusion.2
  51.6 0.1 select_multiply_fusion.2
  51.7 3.6 %collective-permute-start.1 = (f32[128,48]{1,0:T(8,128)S(1)}, f32[128,48]{1,0:T(8,128)S(1)}, u32[]{:S(2)}, u32[]{:S(2)}) collective-permute-start(f32[128,48]{1,0:T(8,128)S(1)} %select_multiply_fusion.2), channel_id=1, source_target_pairs={{0,504},{8,0},{16,8},{24,16},{32,24},{40,32},{48,40},{56,48},{64,5... | collective-permute-start | bytes 73736 | tf_op jit(solution)/shard_map/ppermute | solution.py:12
  55.4 0.6 gather_fusion.3
  56.1 0.1 select_multiply_fusion.1
  56.2 8.0 %collective-permute-start.2 = (f32[128,48]{1,0:T(8,128)S(1)}, f32[128,48]{1,0:T(8,128)S(1)}, u32[]{:S(2)}, u32[]{:S(2)}) collective-permute-start(f32[128,48]{1,0:T(8,128)S(1)} %select_multiply_fusion.1), channel_id=1, source_target_pairs={{0,16},{8,24},{16,32},{24,40},{32,48},{40,56},{48,64},{56,72},{64,... | collective-permute-start | bytes 73736 | tf_op jit(solution)/shard_map/ppermute | solution.py:12
  64.2 0.6 gather_fusion.4
  64.8 0.1 select_multiply_fusion
  65.0 1.9 %collective-permute-start.3 = (f32[128,48]{1,0:T(8,128)S(1)}, f32[128,48]{1,0:T(8,128)S(1)}, u32[]{:S(2)}, u32[]{:S(2)}) collective-permute-start(f32[128,48]{1,0:T(8,128)S(1)} %select_multiply_fusion), channel_id=1, source_target_pairs={{0,496},{8,504},{16,0},{24,8},{32,16},{40,24},{48,32},{56,40},{64,... | collective-permute-start | bytes 73736 | tf_op jit(solution)/shard_map/ppermute | solution.py:12
  67.2 0.1 slice_reduce_fusion.7
  67.4 5.9 %collective-permute-done.3 = f32[128,48]{1,0:T(8,128)S(1)} collective-permute-done((f32[128,48]{1,0:T(8,128)S(1)}, f32[128,48]{1,0:T(8,128)S(1)}, u32[]{:S(2)}, u32[]{:S(2)}) %collective-permute-start.3) | collective-permute-done | bytes 24608 | tf_op jit(solution)/shard_map/ppermute | solution.py:12
  73.2 27.7 %gather_fusion = f32[8192,48]{1,0:T(8,128)} fusion(f32[1536,48]{1,0:T(8,128)S(1)} %constant_dynamic-update-slice_fusion, s32[8192]{0:T(1024)S(1)} %broadcast_clamp_fusion), kind=kCustom, calls=%fused_computation.4 | custom fusion | bytes 3178496 | tf_op jit(solution)/shard_map/jit(_take)/gather | solution.py:28
  100.9 2.8 %copy.29 = f32[8192,48]{0,1:T(8,128)S(1)} copy(f32[8192,48]{1,0:T(8,128)} %gather_fusion) | data formatting | bytes 3145728 | tf_op jit(solution)/shard_map/jit(_take)/gather | solution.py:28
  103.7 0.9 copy.32
  104.7 1.0 fusion
  105.7 0.6 fusion.68
  106.3 34.8 %all_gather.6 = bf16[128,1024]{1,0:T(8,128)(2,1)S(1)} all-gather(bf16[16,1024]{1,0:T(8,128)(2,1)S(1)} %get-tuple-element.15), channel_id=1, replica_groups=mesh['dom'=64,'bin'=8] {'bin'}, dimensions={0}, use_global_device_ids=true | all-gather | bytes 294912 | tf_op jit(solution)/shard_map/all_gather | solution.py:101
  141.1 0.2 fusion.1
  141.3 34.7 %all_gather.7 = bf16[128,1024]{1,0:T(8,128)(2,1)S(1)} all-gather(bf16[16,1024]{1,0:T(8,128)(2,1)S(1)} %fusion.1), channel_id=1, replica_groups=mesh['dom'=64,'bin'=8] {'bin'}, dimensions={0}, use_global_device_ids=true | all-gather | bytes 294912 | tf_op jit(solution)/shard_map/all_gather | solution.py:108
  175.9 1.5 convolution_add_fusion
  (37 shorter events, 0.4 us)
Async XLA Ops:
  0.6 140.5 %copy-start = (bf16[128,128]{1,0:T(8,128)(2,1)S(1)}, bf16[128,128]{1,0:T(8,128)(2,1)}, u32[]{:S(2)}) copy-start(bf16[128,128]{1,0:T(8,128)(2,1)} %param.24) | copy-start | bytes 98308
  46.2 9.9 %copy-start.5 = (f32[2,1024]{1,0:T(2,128)}, f32[2,1024]{1,0:T(2,128)S(1)}, u32[]{:S(2)}) copy-start(f32[2,1024]{1,0:T(2,128)S(1)} %fusion.52) | copy-start | bytes 24580
  47.1 58.6 %copy-start.1 = (f32[2,16,1024]{2,1,0:T(8,128)}, f32[2,16,1024]{2,1,0:T(8,128)S(1)}, u32[]{:S(2)}) copy-start(f32[2,16,1024]{2,1,0:T(8,128)S(1)} %add_divide_fusion) | copy-start | bytes 393220
  49.0 18.3 %collective-permute-start = (f32[128,48]{1,0:T(8,128)S(1)}, f32[128,48]{1,0:T(8,128)S(1)}, u32[]{:S(2)}, u32[]{:S(2)}) collective-permute-start(f32[128,48]{1,0:T(8,128)S(1)} %select_multiply_fusion.3), channel_id=1, source_target_pairs={{0,8},{8,16},{16,24},{24,32},{32,40},{40,48},{48,56},{56,64},{64,7... | collective-permute-start | bytes 73736 | tf_op jit(solution)/shard_map/ppermute | solution.py:12
  51.0 16.0 %copy-start.3 = (s32[8,1024]{1,0:T(8,128)S(1)}, s32[8,1024]{1,0:T(8,128)}, u32[]{:S(2)}) copy-start(s32[8,1024]{1,0:T(8,128)} %param.22) | copy-start | bytes 98308
  51.6 15.4 %copy-start.4 = (f32[2,8,1024]{2,1,0:T(8,128)S(1)}, f32[2,8,1024]{2,1,0:T(8,128)}, u32[]{:S(2)}) copy-start(f32[2,8,1024]{2,1,0:T(8,128)} %param.18) | copy-start | bytes 196612
  51.7 15.6 %collective-permute-start.1 = (f32[128,48]{1,0:T(8,128)S(1)}, f32[128,48]{1,0:T(8,128)S(1)}, u32[]{:S(2)}, u32[]{:S(2)}) collective-permute-start(f32[128,48]{1,0:T(8,128)S(1)} %select_multiply_fusion.2), channel_id=1, source_target_pairs={{0,504},{8,0},{16,8},{24,16},{32,24},{40,32},{48,40},{56,48},{64,5... | collective-permute-start | bytes 73736 | tf_op jit(solution)/shard_map/ppermute | solution.py:12
  56.2 11.2 %collective-permute-start.2 = (f32[128,48]{1,0:T(8,128)S(1)}, f32[128,48]{1,0:T(8,128)S(1)}, u32[]{:S(2)}, u32[]{:S(2)}) collective-permute-start(f32[128,48]{1,0:T(8,128)S(1)} %select_multiply_fusion.1), channel_id=1, source_target_pairs={{0,16},{8,24},{16,32},{24,40},{32,48},{40,56},{48,64},{56,72},{64,... | collective-permute-start | bytes 73736 | tf_op jit(solution)/shard_map/ppermute | solution.py:12
  65.0 8.3 %collective-permute-start.3 = (f32[128,48]{1,0:T(8,128)S(1)}, f32[128,48]{1,0:T(8,128)S(1)}, u32[]{:S(2)}, u32[]{:S(2)}) collective-permute-start(f32[128,48]{1,0:T(8,128)S(1)} %select_multiply_fusion), channel_id=1, source_target_pairs={{0,496},{8,504},{16,0},{24,8},{32,16},{40,24},{48,32},{56,40},{64,... | collective-permute-start | bytes 73736 | tf_op jit(solution)/shard_map/ppermute | solution.py:12
  104.6 1.1 copy-start.2
  104.7 1.1 copy-start.6
  105.7 35.4 %copy-start.7 = (f32[1024]{0:T(1024)S(1)}, f32[1024]{0:T(1024)}, u32[]{:S(2)}) copy-start(f32[1024]{0:T(1024)} %param.20) | copy-start | bytes 12292
where the time goes:
time: 178 us; the launch traced here: 177 us
  blocking collectives  111 us (62%)
  local copies, waits for them, and re-layouts  34.5 us (19%)
  starting transfers between devices  15.5 us (9%)
  other arithmetic  8.26 us (5%)
  waiting for transfers between devices  5.86 us (3%)
    psum x1, blocking collectives, body(): totals = lax.psum(partial_sums, 'bin')  41.3 us
    all_gather x1, blocking collectives, body(): lax.all_gather(rounded, 'bin', axis=0, tiled=True)  34.8 us
    all_gather x1, blocking collectives, body(): lax.all_gather(loss, 'bin', axis=0, tiled=True)  34.7 us
    gather x2, local copies, waits for them, and re-layouts, advect(): picked = jnp.take(extended_rows, safe_all, axis=0)  30.5 us
    ppermute x4, starting transfers between devices, from_behind(): return lax.ppermute(value, axis, pairs)  15.5 us
    ppermute x4, waiting for transfers between devices, from_behind(): return lax.ppermute(value, axis, pairs)  5.86 us
  transfers between devices with their start and end apart: 4, of which 1 were waited for; matrix products, arithmetic and copies ran while one was open for 1% of the time, Pallas kernels for 0%

commit v1 on v0

--- a/solution.py
+++ b/solution.py
@@ -1,9 +1,20 @@
+import functools
 import jax
 import jax.numpy as jnp
 from jax import lax
 from jax.sharding import PartitionSpec as P
 
 OFFSETS = (1, -1, 2, -2)
+
+
+def _spread_rings(packet, mesh_ax, pos_dim):
+    before = lax.axis_size(mesh_ax)
+    tall = jnp.stack([packet] * before)
+    tile_out = lax.all_to_all(tall, mesh_ax, 0, 0)
+    return jnp.concatenate(tile_out, axis=pos_dim)
+
+
+group_clear = functools.partial(_spread_rings, mesh_ax="bin", pos_dim=0)
 
 
 def from_behind(value, axis, steps):
@@ -96,11 +107,7 @@
     first_bin = lax.axis_index("bin") * own_rows
     kernel_rows = lax.dynamic_slice_in_dim(kernel, first_bin, own_rows, 0)
     columns = kernel_rows
-    collide = jnp.dot(
-        columns,
-        lax.all_gather(rounded, "bin", axis=0, tiled=True),
-        preferred_element_type=jnp.float32,
-    )
+    collide = jnp.dot(columns, group_clear(rounded), preferred_element_type=jnp.float32)
     loss = (coag_rate[None, :] * rounded.astype(jnp.float32) * collide).astype(jnp.bfloat16)
     redis_rows = lax.dynamic_slice_in_dim(redistrib, first_bin, own_rows, 0)
     columns = redis_rows

time: 178 us -> 157 us (0.88)
  blocking collectives: 111 us -> 76.2 us
  waiting for transfers between devices: 5.86 us -> 14.6 us
  starting transfers between devices: 15.5 us -> 18.9 us
    all_gather x1 -> x0, blocking collectives: 34.8 us -> none  [body(): lax.all_gather(rounded, 'bin', axis=0, tiled=True)]
    all_to_all x0 -> x1, waiting for transfers between devices: none -> 8.72 us  [_spread_rings(): tile_out = lax.all_to_all(tall, mesh_ax, 0, 0)]
    all_to_all x0 -> x1, starting transfers between devices: none -> 3.41 us  [_spread_rings(): tile_out = lax.all_to_all(tall, mesh_ax, 0, 0)]
  transfers between devices with their start and end apart: 4 -> 5, of which waited for: 1 -> 2; matrix products, arithmetic and copies ran while one was open for 1% -> 2% of each run, Pallas kernels for 0% -> 0%
where the time goes in v1:
time: 157 us; the launch traced here: 156 us
  blocking collectives  76.2 us (49%)
  local copies, waits for them, and re-layouts  35.2 us (22%)
  starting transfers between devices  18.9 us (12%)
  waiting for transfers between devices  14.6 us (9%)
  other arithmetic  8.26 us (5%)
  matrix products  1.62 us (1%)
    psum x1, blocking collectives, body(): totals = lax.psum(partial_sums, 'bin')  41.3 us
    all_gather x1, blocking collectives, body(): lax.all_gather(loss, 'bin', axis=0, tiled=True)  35 us
    gather x2, local copies, waits for them, and re-layouts, advect(): picked = jnp.take(extended_rows, safe_all, axis=0)  30.5 us
    ppermute x4, starting transfers between devices, from_behind(): return lax.ppermute(value, axis, pairs)  15.5 us
    all_to_all x1, waiting for transfers between devices, _spread_rings(): tile_out = lax.all_to_all(tall, mesh_ax, 0, 0)  8.72 us
    ppermute x4, waiting for transfers between devices, from_behind(): return lax.ppermute(value, axis, pairs)  5.86 us
    all_to_all x1, starting transfers between devices, _spread_rings(): tile_out = lax.all_to_all(tall, mesh_ax, 0, 0)  3.41 us
  transfers between devices with their start and end apart: 5, of which 2 were waited for; matrix products, arithmetic and copies ran while one was open for 2% of the time, Pallas kernels for 0%

profile of v1, /device:TPU:98, one launch (start us, length us, event | category | flops | bytes accessed | tf_op | source)
XLA Modules:
  0.0 155.8 jit_solution(11632626445815436158)
XLA Ops:
  0.6 0.8 compare_and_fusion
  1.5 0.8 fusion.65
  2.3 1.0 broadcast_multiply_fusion
  3.3 0.9 fusion.51
  4.2 41.3 %psum.7 = f32[3,1024]{1,0:T(4,128)S(1)} all-reduce(f32[3,1024]{1,0:T(4,128)S(1)} %pad_maximum_fusion.1), channel_id=1, replica_groups=mesh['dom'=64,'bin'=8] {'bin'}, use_global_device_ids=true, to_apply=%region_3.0 | all-reduce | flops 3072 | bytes 24576 | tf_op jit(solution)/shard_map/psum | solution.py:91
  45.5 0.7 fusion.52
  46.2 0.9 add_divide_fusion
  47.2 0.9 pad_maximum_fusion
  48.1 0.2 copy.28
  48.3 0.6 gather_fusion.1
  49.0 1.9 %collective-permute-start = (f32[128,48]{1,0:T(8,128)S(1)}, f32[128,48]{1,0:T(8,128)S(1)}, u32[]{:S(2)}, u32[]{:S(2)}) collective-permute-start(f32[128,48]{1,0:T(8,128)S(1)} %select_multiply_fusion.3), channel_id=1, source_target_pairs={{0,8},{8,16},{16,24},{24,32},{32,40},{40,48},{48,56},{56,64},{64,7... | collective-permute-start | bytes 73736 | tf_op jit(solution)/shard_map/ppermute | solution.py:23
  51.0 0.6 gather_fusion.2
  51.6 0.1 select_multiply_fusion.2
  51.7 3.6 %collective-permute-start.1 = (f32[128,48]{1,0:T(8,128)S(1)}, f32[128,48]{1,0:T(8,128)S(1)}, u32[]{:S(2)}, u32[]{:S(2)}) collective-permute-start(f32[128,48]{1,0:T(8,128)S(1)} %select_multiply_fusion.2), channel_id=1, source_target_pairs={{0,504},{8,0},{16,8},{24,16},{32,24},{40,32},{48,40},{56,48},{64,5... | collective-permute-start | bytes 73736 | tf_op jit(solution)/shard_map/ppermute | solution.py:23
  55.4 0.6 gather_fusion.3
  56.1 0.1 select_multiply_fusion.1
  56.2 8.0 %collective-permute-start.2 = (f32[128,48]{1,0:T(8,128)S(1)}, f32[128,48]{1,0:T(8,128)S(1)}, u32[]{:S(2)}, u32[]{:S(2)}) collective-permute-start(f32[128,48]{1,0:T(8,128)S(1)} %select_multiply_fusion.1), channel_id=1, source_target_pairs={{0,16},{8,24},{16,32},{24,40},{32,48},{40,56},{48,64},{56,72},{64,... | collective-permute-start | bytes 73736 | tf_op jit(solution)/shard_map/ppermute | solution.py:23
  64.2 0.6 gather_fusion.4
  65.0 1.9 %collective-permute-start.3 = (f32[128,48]{1,0:T(8,128)S(1)}, f32[128,48]{1,0:T(8,128)S(1)}, u32[]{:S(2)}, u32[]{:S(2)}) collective-permute-start(f32[128,48]{1,0:T(8,128)S(1)} %select_multiply_fusion), channel_id=1, source_target_pairs={{0,496},{8,504},{16,0},{24,8},{32,16},{40,24},{48,32},{56,40},{64,... | collective-permute-start | bytes 73736 | tf_op jit(solution)/shard_map/ppermute | solution.py:23
  67.2 0.1 slice_reduce_fusion.7
  67.4 5.9 %collective-permute-done.3 = f32[128,48]{1,0:T(8,128)S(1)} collective-permute-done((f32[128,48]{1,0:T(8,128)S(1)}, f32[128,48]{1,0:T(8,128)S(1)}, u32[]{:S(2)}, u32[]{:S(2)}) %collective-permute-start.3) | collective-permute-done | bytes 24608 | tf_op jit(solution)/shard_map/ppermute | solution.py:23
  73.2 27.7 %gather_fusion = f32[8192,48]{1,0:T(8,128)} fusion(f32[1536,48]{1,0:T(8,128)S(1)} %constant_dynamic-update-slice_fusion, s32[8192]{0:T(1024)S(1)} %broadcast_clamp_fusion), kind=kCustom, calls=%fused_computation.4 | custom fusion | bytes 3178496 | tf_op jit(solution)/shard_map/jit(_take)/gather | solution.py:39
  100.9 2.8 %copy.29 = f32[8192,48]{0,1:T(8,128)S(1)} copy(f32[8192,48]{1,0:T(8,128)} %gather_fusion) | data formatting | bytes 3145728 | tf_op jit(solution)/shard_map/jit(_take)/gather | solution.py:39
  103.7 0.9 copy.32
  104.7 1.0 fusion
  105.7 0.6 fusion.68
  106.3 0.7 stack.27
  107.1 3.4 %all-to-all-start = ((bf16[8,16,1024]{2,1,0:T(8,128)(2,1)}), bf16[8,16,1024]{2,1,0:T(8,128)(2,1)S(1)}, u32[]{:S(2)}, u32[]{:S(2)}) async-start(bf16[8,16,1024]{2,1,0:T(8,128)(2,1)} %stack.27), calls=%async_computation | async-start | bytes 524288 | tf_op jit(solution)/shard_map/all_to_all | solution.py:13
  110.5 8.7 %all-to-all-done = bf16[8,16,1024]{2,1,0:T(8,128)(2,1)S(1)} async-done(((bf16[8,16,1024]{2,1,0:T(8,128)(2,1)}), bf16[8,16,1024]{2,1,0:T(8,128)(2,1)S(1)}, u32[]{:S(2)}, u32[]{:S(2)}) %all-to-all-start) | async-done | bytes 262176 | tf_op jit(solution)/shard_map/all_to_all | solution.py:13
  119.2 0.2 fusion.1
  119.4 35.0 %all_gather.3 = bf16[128,1024]{1,0:T(8,128)(2,1)S(1)} all-gather(bf16[16,1024]{1,0:T(8,128)(2,1)S(1)} %fusion.1), channel_id=1, replica_groups=mesh['dom'=64,'bin'=8] {'bin'}, dimensions={0}, use_global_device_ids=true | all-gather | bytes 294912 | tf_op jit(solution)/shard_map/all_gather | solution.py:115
  154.3 1.5 convolution_add_fusion
  (39 shorter events, 0.6 us)
Async XLA Ops:
  0.6 118.6 %copy-start = (bf16[128,128]{1,0:T(8,128)(2,1)S(1)}, bf16[128,128]{1,0:T(8,128)(2,1)}, u32[]{:S(2)}) copy-start(bf16[128,128]{1,0:T(8,128)(2,1)} %param.24) | copy-start | bytes 98308
  46.2 9.9 %copy-start.5 = (f32[2,1024]{1,0:T(2,128)}, f32[2,1024]{1,0:T(2,128)S(1)}, u32[]{:S(2)}) copy-start(f32[2,1024]{1,0:T(2,128)S(1)} %fusion.52) | copy-start | bytes 24580
  47.1 58.6 %copy-start.1 = (f32[2,16,1024]{2,1,0:T(8,128)}, f32[2,16,1024]{2,1,0:T(8,128)S(1)}, u32[]{:S(2)}) copy-start(f32[2,16,1024]{2,1,0:T(8,128)S(1)} %add_divide_fusion) | copy-start | bytes 393220
  49.0 18.3 %collective-permute-start = (f32[128,48]{1,0:T(8,128)S(1)}, f32[128,48]{1,0:T(8,128)S(1)}, u32[]{:S(2)}, u32[]{:S(2)}) collective-permute-start(f32[128,48]{1,0:T(8,128)S(1)} %select_multiply_fusion.3), channel_id=1, source_target_pairs={{0,8},{8,16},{16,24},{24,32},{32,40},{40,48},{48,56},{56,64},{64,7... | collective-permute-start | bytes 73736 | tf_op jit(solution)/shard_map/ppermute | solution.py:23
  51.0 16.0 %copy-start.3 = (s32[8,1024]{1,0:T(8,128)S(1)}, s32[8,1024]{1,0:T(8,128)}, u32[]{:S(2)}) copy-start(s32[8,1024]{1,0:T(8,128)} %param.22) | copy-start | bytes 98308
  51.6 15.4 %copy-start.4 = (f32[2,8,1024]{2,1,0:T(8,128)S(1)}, f32[2,8,1024]{2,1,0:T(8,128)}, u32[]{:S(2)}) copy-start(f32[2,8,1024]{2,1,0:T(8,128)} %param.18) | copy-start | bytes 196612
  51.7 15.6 %collective-permute-start.1 = (f32[128,48]{1,0:T(8,128)S(1)}, f32[128,48]{1,0:T(8,128)S(1)}, u32[]{:S(2)}, u32[]{:S(2)}) collective-permute-start(f32[128,48]{1,0:T(8,128)S(1)} %select_multiply_fusion.2), channel_id=1, source_target_pairs={{0,504},{8,0},{16,8},{24,16},{32,24},{40,32},{48,40},{56,48},{64,5... | collective-permute-start | bytes 73736 | tf_op jit(solution)/shard_map/ppermute | solution.py:23
  56.2 11.2 %collective-permute-start.2 = (f32[128,48]{1,0:T(8,128)S(1)}, f32[128,48]{1,0:T(8,128)S(1)}, u32[]{:S(2)}, u32[]{:S(2)}) collective-permute-start(f32[128,48]{1,0:T(8,128)S(1)} %select_multiply_fusion.1), channel_id=1, source_target_pairs={{0,16},{8,24},{16,32},{24,40},{32,48},{40,56},{48,64},{56,72},{64,... | collective-permute-start | bytes 73736 | tf_op jit(solution)/shard_map/ppermute | solution.py:23
  65.0 8.3 %collective-permute-start.3 = (f32[128,48]{1,0:T(8,128)S(1)}, f32[128,48]{1,0:T(8,128)S(1)}, u32[]{:S(2)}, u32[]{:S(2)}) collective-permute-start(f32[128,48]{1,0:T(8,128)S(1)} %select_multiply_fusion), channel_id=1, source_target_pairs={{0,496},{8,504},{16,0},{24,8},{32,16},{40,24},{48,32},{56,40},{64,... | collective-permute-start | bytes 73736 | tf_op jit(solution)/shard_map/ppermute | solution.py:23
  104.6 1.1 copy-start.2
  104.7 1.1 copy-start.6
  105.7 13.5 %copy-start.7 = (f32[1024]{0:T(1024)S(1)}, f32[1024]{0:T(1024)}, u32[]{:S(2)}) copy-start(f32[1024]{0:T(1024)} %param.20) | copy-start | bytes 12292
  107.1 12.1 %all-to-all-start = ((bf16[8,16,1024]{2,1,0:T(8,128)(2,1)}), bf16[8,16,1024]{2,1,0:T(8,128)(2,1)S(1)}, u32[]{:S(2)}, u32[]{:S(2)}) async-start(bf16[8,16,1024]{2,1,0:T(8,128)(2,1)} %stack.27), calls=%async_computation | async-start | bytes 524288 | tf_op jit(solution)/shard_map/all_to_all | solution.py:13
